TPU v7x, 256 devices: a whole 4x4x8 slice. The times are simulated.
256 devices in a mesh: rec: 32 (over z, y), src: 8 (over x, core).
Axes of the slice: x: 4, y: 4, z: 8, core: 2. Of those that a mesh axis runs over, the one named last changes fastest.
Arguments:
- kernel: float32 [2, 2, 5120, 5120], P(None, None, 'rec', 'src'), may hold values from -0.0625 to 0.0625
- traces: float32 [8, 896, 2, 2, 256], P('src', 'rec')
- acq_lists: int32 [8, 896], P('src', 'rec'), may hold values from 0 to 639, as said below
- counts: int32 [8, 32], P('src', 'rec'), may hold values from 1 to 28, as said below
Outputs:
- solution: float32 [5120, 2, 2, 256], P(('src', 'rec'))
- next_left: float32 [5120, 2, 2, 256], P(('rec', 'src'))
Inputs may be any that keep to these rules, and one draw needn't show every extreme that they name: `acq_lists`: an id a * 20 + k names row k of area a. Within each list the first counts[s, r] slots of the blocks name every id exactly once; other slots hold ids to be ignored. No block names more than 1 ids of one area, and every block that names an area names exactly 1 of its ids. `counts`: used slots of a block; in every list some block uses all 28.
All inputs are finite; a program needn't handle non-finite values.
Results may differ from a plain program's by a relative error of at most 0.00026.
Values sent between devices are 32-bit elements; how exact they have to be, the bound alone decides.
A program may use at most 64 MiB of HBM per device.

v0:
```python
import jax
import jax.numpy as jnp
from jax import lax
from jax.sharding import PartitionSpec as P

NR = 5120
FREQS = 2
SOURCES = 256
ITERS = 2


def kernel_apply(kernel, vector):
    highest = lax.Precision.HIGHEST
    real_part = jnp.einsum("fmc,cfn->mfn", kernel[0], vector[:, 0], precision=highest) - jnp.einsum(
        "fmc,cfn->mfn", kernel[1], vector[:, 1], precision=highest
    )
    imag_part = jnp.einsum("fmc,cfn->mfn", kernel[0], vector[:, 1], precision=highest) + jnp.einsum(
        "fmc,cfn->mfn", kernel[1], vector[:, 0], precision=highest
    )
    return jnp.stack([real_part, imag_part], axis=1)


def kernel_adjoint(kernel, vector):
    highest = lax.Precision.HIGHEST
    real_part = jnp.einsum("fmc,mfn->cfn", kernel[0], vector[:, 0], precision=highest) + jnp.einsum(
        "fmc,mfn->cfn", kernel[1], vector[:, 1], precision=highest
    )
    imag_part = jnp.einsum("fmc,mfn->cfn", kernel[0], vector[:, 1], precision=highest) - jnp.einsum(
        "fmc,mfn->cfn", kernel[1], vector[:, 0], precision=highest
    )
    return jnp.stack([real_part, imag_part], axis=1)


def widen(values):
    return values[None, None, :, None]


def rms_norm(vector):
    local_sum = jnp.sum(vector * vector, axis=(0, 1, 3))
    global_sum = lax.psum(local_sum, ("rec", "src"))
    return jnp.sqrt(global_sum / (2.0 * NR * SOURCES))


def on_device(kernel, traces, acq_lists, counts):
    highest = lax.Precision.HIGHEST
    my_area = lax.axis_index("rec")
    row_count = kernel.shape[2] // lax.axis_size("src")
    slot_count = traces.shape[1]
    width = traces.shape[2] * traces.shape[3] * traces.shape[4]
    row_iota = jnp.arange(row_count, dtype=jnp.int32)
    piece_traces = lax.all_gather(traces, "rec", axis=1, tiled=True)
    piece_ids = lax.all_gather(acq_lists, "rec", axis=1, tiled=True)
    piece_counts = lax.all_gather(counts, "rec", axis=1, tiled=True)
    span_slots = piece_ids.shape[1]
    slot_iota = jnp.arange(span_slots, dtype=jnp.int32)
    block_iota = jnp.arange(piece_counts.shape[1], dtype=jnp.int32)
    in_block = (slot_iota // slot_count)[:, None] == block_iota[None, :]
    limits = jnp.sum(jnp.where(in_block, piece_counts[0][None, :], 0), axis=1)
    filled = slot_iota % slot_count < limits
    list_ids = piece_ids[0]
    wanted = filled & (list_ids // row_count == my_area)
    selector = ((list_ids % row_count)[None, :] == row_iota[:, None]) & wanted[None, :]
    observed = jnp.dot(
        selector.astype(jnp.float32), piece_traces.reshape(span_slots, width), precision=highest
    )
    observed = observed.reshape(row_count, 2, FREQS, SOURCES)

    def adjoint(vector):
        spread = lax.all_gather(vector, "src", axis=0, tiled=True)
        return lax.psum_scatter(
            kernel_adjoint(kernel, spread), "rec", scatter_dimension=0, tiled=True
        )

    beta_norm = rms_norm(observed)
    left_unit = observed / widen(beta_norm)
    right_vec = adjoint(left_unit)
    alpha_norm = rms_norm(right_vec)
    right_unit = right_vec / widen(alpha_norm)
    search = right_unit
    solution = jnp.zeros(right_unit.shape, jnp.float32)
    phibar = beta_norm
    rhobar = alpha_norm
    next_left = observed
    for iteration in range(ITERS):
        forward_spread = lax.all_gather(right_unit, "rec", axis=0, tiled=True)
        next_left = (
            lax.psum_scatter(
                kernel_apply(kernel, forward_spread), "src", scatter_dimension=0, tiled=True
            )
            - widen(alpha_norm) * left_unit
        )
        beta_norm = rms_norm(next_left)
        left_unit = next_left / widen(beta_norm)
        rho_value = jnp.sqrt(rhobar * rhobar + beta_norm * beta_norm)
        cosine = rhobar / rho_value
        sine_value = beta_norm / rho_value
        phi_value = cosine * phibar
        phibar = sine_value * phibar
        solution = solution + widen(phi_value / rho_value) * search
        if iteration + 1 < ITERS:
            right_vec = adjoint(left_unit) - widen(beta_norm) * right_unit
            alpha_norm = rms_norm(right_vec)
            right_unit = right_vec / widen(alpha_norm)
            theta_value = sine_value * alpha_norm
            rhobar = -cosine * alpha_norm
            search = right_unit - widen(theta_value / rho_value) * search
    return (solution, next_left)


def solution(mesh):
    placed = (
        P(None, None, "rec", "src"),
        P("src", "rec", None, None, None),
        P("src", "rec"),
        P("src", "rec"),
    )
    return jax.shard_map(
        on_device,
        mesh=mesh,
        in_specs=placed,
        out_specs=(P(("src", "rec"), None, None, None), P(("rec", "src"), None, None, None)),
        check_vma=False,
    )
```

profile of v0, /device:TPU:1, one launch (start us, length us, event | category | flops | bytes accessed | tf_op | source)
XLA Modules:
  0.0 1147.3 jit_solution(5020311262918664336)
XLA Ops:
  7.2 0.7 all-gather.4.cloned.1.call-update
  8.6 1.3 fusion.76
  11.3 0.8 bitcast_dynamic-update-slice_fusion.1
  12.1 20.3 %all-reduce.6 = (s32[896]{0:T(1024)S(1)}, s32[32]{0:T(128)S(1)}) all-reduce(s32[896]{0:T(1024)S(1)} %bitcast_dynamic-update-slice_fusion.1, s32[32]{0:T(128)S(1)} %bitcast_dynamic-update-slice_fusion), channel_id=1, replica_groups=mesh['rec'=32,'src'=8] {'rec'}, use_global_device_ids=true, to_apply=%add | all-reduce | flops 928 | bytes 7424
  32.6 59.6 %all-gather.4.cloned.1.call-done = f32[1,896,2,2,256]{4,3,2,0,1:T(2,128)} async-done(((f32[1,28,2,2,256]{4,3,2,0,1:T(2,128)}), f32[1,896,2,2,256]{4,3,2,0,1:T(2,128)}) %all-gather.4.cloned.1.call-update) | async-done | bytes 3670032 | tf_op jit(solution)/shard_map/all_gather | solution.py:51
  92.1 6.6 copy.66
  98.8 3.9 multiply_reduce_fusion.3
  102.7 77.6 %psum.35 = f32[2]{0:T(128)S(1)} all-reduce(f32[2]{0:T(128)S(1)} %get-tuple-element.32), channel_id=1, replica_groups=mesh['rec'=32,'src'=8] {'rec','src'}, use_global_device_ids=true, to_apply=%region_2.3 | all-reduce | flops 2 | bytes 16 | tf_op jit(solution)/shard_map/psum | solution.py:40
  180.4 14.0 %all_gather.24 = f32[160,2,2,256]{3,2,1,0:T(2,128)S(1)} all-gather(f32[20,2,2,256]{3,2,1,0:T(2,128)S(1)} %copy.43), channel_id=1, replica_groups=mesh['rec'=32,'src'=8] {'src'}, dimensions={0}, use_global_device_ids=true | all-gather | bytes 737280 | tf_op jit(solution)/shard_map/all_gather | solution.py:69
  194.7 1.4 fusion.38
  196.1 1.4 fusion.40
  197.6 1.5 fusion.4
  199.1 1.5 fusion.5
  200.6 1.7 pad_maximum_fusion
  202.3 5.1 copy.46
  208.2 146.3 %all-reduce.12.cloned.1.call-done = f32[640,2,2,256]{3,2,1,0:T(2,128)} async-done(((f32[640,2,2,256]{3,2,1,0:T(2,128)}), f32[640,2,2,256]{3,2,1,0:T(2,128)}) %all-reduce.12.cloned.1.call-update) | async-done | bytes 2621456
  354.5 1.1 multiply_reduce_fusion.4
  355.6 78.4 %psum.36 = f32[2]{0:T(128)S(1)} all-reduce(f32[2]{0:T(128)S(1)} %get-tuple-element.17), channel_id=1, replica_groups=mesh['rec'=32,'src'=8] {'rec','src'}, use_global_device_ids=true, to_apply=%region_5.6 | all-reduce | flops 2 | bytes 16 | tf_op jit(solution)/shard_map/psum | solution.py:40
  435.0 71.0 %all-gather.6.cloned.1.call-done = f32[640,2,2,256]{3,2,1,0:T(2,128)} async-done(((f32[20,2,2,256]{3,2,1,0:T(2,128)}), f32[640,2,2,256]{3,2,1,0:T(2,128)}) %all-gather.6.cloned.1.call-update) | async-done | bytes 2621456 | tf_op jit(solution)/shard_map/all_gather | solution.py:85
  506.0 2.6 fusion.73
  508.7 1.1 fusion.6
  509.8 1.1 fusion.7
  511.0 1.1 fusion.21
  512.1 1.1 fusion.19
  513.3 1.4 copy.51
  516.0 63.6 %all-reduce.14.cloned.1.call-done = f32[160,2,2,256]{3,2,1,0:T(2,128)} async-done(((f32[160,2,2,256]{3,2,1,0:T(2,128)}), f32[160,2,2,256]{3,2,1,0:T(2,128)}) %all-reduce.14.cloned.1.call-update) | async-done | bytes 655376
  579.6 0.9 constant_dynamic-slice_fusion.2
  580.7 78.5 %psum.37 = f32[2]{0:T(128)S(1)} all-reduce(f32[2]{0:T(128)S(1)} %multiply_reduce_fusion.2), channel_id=1, replica_groups=mesh['rec'=32,'src'=8] {'rec','src'}, use_global_device_ids=true, to_apply=%region_8.9 | all-reduce | flops 2 | bytes 16 | tf_op jit(solution)/shard_map/psum | solution.py:40
  659.4 14.2 %all_gather.26 = f32[160,2,2,256]{3,2,1,0:T(2,128)S(1)} all-gather(f32[20,2,2,256]{3,2,1,0:T(2,128)S(1)} %copy.53), channel_id=1, replica_groups=mesh['rec'=32,'src'=8] {'src'}, dimensions={0}, use_global_device_ids=true | all-gather | bytes 737280 | tf_op jit(solution)/shard_map/all_gather | solution.py:69
  673.8 1.4 fusion.32
  675.2 1.4 fusion.34
  676.7 1.5 fusion.2
  678.2 1.5 fusion.3
  679.7 1.7 pad_maximum_fusion.1
  681.4 5.1 copy.56
  686.6 147.7 %all-reduce.16.cloned.1.call-done = f32[640,2,2,256]{3,2,1,0:T(2,128)} async-done(((f32[640,2,2,256]{3,2,1,0:T(2,128)}), f32[640,2,2,256]{3,2,1,0:T(2,128)}) %all-reduce.16.cloned.1.call-update) | async-done | bytes 2621456
  834.3 0.9 constant_dynamic-slice_fusion.1
  835.4 78.4 %psum.38 = f32[2]{0:T(128)S(1)} all-reduce(f32[2]{0:T(128)S(1)} %multiply_reduce_fusion.1), channel_id=1, replica_groups=mesh['rec'=32,'src'=8] {'rec','src'}, use_global_device_ids=true, to_apply=%region_11.12 | all-reduce | flops 2 | bytes 16 | tf_op jit(solution)/shard_map/psum | solution.py:40
  914.9 70.9 %all-gather.8.cloned.1.call-done = f32[640,2,2,256]{3,2,1,0:T(2,128)} async-done(((f32[20,2,2,256]{3,2,1,0:T(2,128)}), f32[640,2,2,256]{3,2,1,0:T(2,128)}) %all-gather.8.cloned.1.call-update) | async-done | bytes 2621456 | tf_op jit(solution)/shard_map/all_gather | solution.py:85
  985.8 2.6 fusion.72
  988.4 1.1 fusion.10
  989.6 1.1 fusion.11
  990.8 1.1 fusion.17
  991.9 1.1 fusion.15
  993.1 1.4 copy.61
  994.5 64.9 %all-reduce.18.cloned.1.call-done = f32[160,2,2,256]{3,2,1,0:T(2,128)} async-done(((f32[160,2,2,256]{3,2,1,0:T(2,128)}), f32[160,2,2,256]{3,2,1,0:T(2,128)}) %all-reduce.18.cloned.1.call-update) | async-done | bytes 655376
  1059.4 0.9 constant_dynamic-slice_fusion
  1060.5 78.5 %psum.39 = f32[2]{0:T(128)S(1)} all-reduce(f32[2]{0:T(128)S(1)} %get-tuple-element.15), channel_id=1, replica_groups=mesh['rec'=32,'src'=8] {'rec','src'}, use_global_device_ids=true, to_apply=%region_14.15 | all-reduce | flops 2 | bytes 16 | tf_op jit(solution)/shard_map/psum | solution.py:40
  (51 shorter events, 6.7 us)
Async XLA Ops:
  7.2 85.0 %all-gather.4.cloned.1.call-start = ((), (), s32[]{:S(2)}) async-start(), calls=%async_computation | async-start | bytes 3784704 | tf_op jit(solution)/shard_map/all_gather | solution.py:51
  7.9 346.6 %all-reduce.12.cloned.1.call-start = ((), (), s32[]{:S(2)}) async-start(), calls=%async_computation.3 | async-start | bytes 5242880
  102.7 92.0 %copy-start = (f32[2,2,160,640]{3,2,1,0:T(8,128)S(1)}, f32[2,2,160,640]{3,2,1,0:T(8,128)}, u32[]{:S(2)}) copy-start(f32[2,2,160,640]{3,2,1,0:T(8,128)} %param.4) | copy-start | bytes 4915204
  207.5 298.6 %all-gather.6.cloned.1.call-start = ((), (), s32[]{:S(2)}) async-start(), calls=%async_computation.1 | async-start | bytes 2703360 | tf_op jit(solution)/shard_map/all_gather | solution.py:85
  434.8 144.9 %all-reduce.14.cloned.1.call-start = ((), (), s32[]{:S(2)}) async-start(), calls=%async_computation.4 | async-start | bytes 1310720
  513.3 1.5 copy-start.1
  514.7 319.6 %all-reduce.16.cloned.1.call-start = ((), (), s32[]{:S(2)}) async-start(), calls=%async_computation.5 | async-start | bytes 5242880
  686.6 299.3 %all-gather.8.cloned.1.call-start = ((), (), s32[]{:S(2)}) async-start(), calls=%async_computation.2 | async-start | bytes 2703360 | tf_op jit(solution)/shard_map/all_gather | solution.py:85
  914.6 144.8 %all-reduce.18.cloned.1.call-start = ((), (), s32[]{:S(2)}) async-start(), calls=%async_computation.6 | async-start | bytes 1310720
Sparse Core Ops, SparseCore 0:
  10.6 81.5 all-gather.3
  207.6 146.8 all-reduce.11
  434.9 71.0 all-gather.5
  514.8 64.7 all-reduce.13
  686.7 147.5 all-reduce.15
  914.7 71.0 all-gather.7
  994.6 64.7 all-reduce.17
where the time goes:
time: 1150 us
  waiting for transfers between devices  625 us (54%)
  blocking collectives  440 us (38%)
  local copies, waits for them, and re-layouts  34.2 us (3%)
  matrix products  24.8 us (2%)
  between operations  17 us (1%)
    unnamed x11, waiting for transfers between devices  423 us
    psum x5, blocking collectives, rms_norm(): global_sum = lax.psum(local_sum, ('rec', 'src'))  391 us
    all_gather x2, waiting for transfers between devices, on_device(): forward_spread = lax.all_gather(right_unit, 'rec', axis=0, tiled=True)  142 us
    all_gather x1, waiting for transfers between devices, on_device(): piece_traces = lax.all_gather(traces, 'rec', axis=1, tiled=True)  59.6 us
    all_gather x2, blocking collectives, adjoint(): spread = lax.all_gather(vector, 'src', axis=0, tiled=True)  28.2 us
  transfers between devices with their start and end apart: 7, of which 7 were waited for; matrix products, arithmetic and copies ran while one was open for 0% of the time, Pallas kernels for 0%

commit v1 on v0

--- a/solution.py
+++ b/solution.py
@@ -82,7 +82,11 @@
     rhobar = alpha_norm
     next_left = observed
     for iteration in range(ITERS):
-        forward_spread = lax.all_gather(right_unit, "rec", axis=0, tiled=True)
+        length = lax.axis_size("rec")
+        repeats = [length if d == 0 else 1 for d in range(right_unit.ndim)]
+        forward_spread = lax.all_to_all(
+            jnp.tile(right_unit, repeats), "rec", split_axis=0, concat_axis=0, tiled=True
+        )
         next_left = (
             lax.psum_scatter(
                 kernel_apply(kernel, forward_spread), "src", scatter_dimension=0, tiled=True

time: 1150 us -> 1140 us (level)
  waiting for transfers between devices: 625 us -> 474 us
  blocking collectives: 440 us -> 574 us
    all_gather x2 -> x0, waiting for transfers between devices: 142 us -> none  [on_device(): forward_spread = lax.all_gather(right_unit, 'rec', axis=0, tiled=True)]
    all_to_all x0 -> x2, blocking collectives: none -> 133 us  [on_device(): lax.all_to_all(jnp.tile(right_unit, repeats), 'rec', split_axis=0, concat...]
    unnamed x11 -> x9, waiting for transfers between devices: 423 us -> 414 us
  transfers between devices with their start and end apart: 7 -> 5, of which waited for: 7 -> 5; matrix products, arithmetic and copies ran while one was open for 0% -> 0% of each run, Pallas kernels for 0% -> 0%
where the time goes in v1:
time: 1140 us; the launch traced here: 1130 us
  blocking collectives  574 us (50%)
  waiting for transfers between devices  474 us (42%)
  local copies, waits for them, and re-layouts  31.8 us (3%)
  matrix products  24.8 us (2%)
  between operations  16.9 us (1%)
    unnamed x9, waiting for transfers between devices  414 us
    psum x5, blocking collectives, rms_norm(): global_sum = lax.psum(local_sum, ('rec', 'src'))  392 us
    all_to_all x2, blocking collectives, on_device(): lax.all_to_all(jnp.tile(right_unit, repeats), 'rec', split_axis=0, concat...  133 us
    all_gather x1, waiting for transfers between devices, on_device(): piece_traces = lax.all_gather(traces, 'rec', axis=1, tiled=True)  59.6 us
    all_gather x2, blocking collectives, adjoint(): spread = lax.all_gather(vector, 'src', axis=0, tiled=True)  28.2 us
  transfers between devices with their start and end apart: 5, of which 5 were waited for; matrix products, arithmetic and copies ran while one was open for 0% of the time, Pallas kernels for 0%

profile of v1, /device:TPU:1, one launch (start us, length us, event | category | flops | bytes accessed | tf_op | source)
XLA Modules:
  0.0 1127.3 jit_solution(918189334637589336)
XLA Ops:
  8.6 1.3 fusion.76
  12.1 20.3 %all-reduce.6 = (s32[896]{0:T(1024)S(1)}, s32[32]{0:T(128)S(1)}) all-reduce(s32[896]{0:T(1024)S(1)} %bitcast_dynamic-update-slice_fusion.1, s32[32]{0:T(128)S(1)} %bitcast_dynamic-update-slice_fusion), channel_id=1, replica_groups=mesh['rec'=32,'src'=8] {'rec'}, use_global_device_ids=true, to_apply=%add | all-reduce | flops 928 | bytes 7424
  32.6 59.6 %all-gather.2.cloned.1.call-done = f32[1,896,2,2,256]{4,3,2,0,1:T(2,128)} async-done(((f32[1,28,2,2,256]{4,3,2,0,1:T(2,128)}), f32[1,896,2,2,256]{4,3,2,0,1:T(2,128)}) %all-gather.2.cloned.1.call-update) | async-done | bytes 3670032 | tf_op jit(solution)/shard_map/all_gather | solution.py:51
  92.1 6.6 copy.81
  98.8 3.9 multiply_reduce_fusion.3
  102.7 77.6 %psum.35 = f32[2]{0:T(128)S(1)} all-reduce(f32[2]{0:T(128)S(1)} %get-tuple-element.34), channel_id=1, replica_groups=mesh['rec'=32,'src'=8] {'rec','src'}, use_global_device_ids=true, to_apply=%region_2.3 | all-reduce | flops 2 | bytes 16 | tf_op jit(solution)/shard_map/psum | solution.py:40
  180.4 14.0 %all_gather.18 = f32[160,2,2,256]{3,2,1,0:T(2,128)S(1)} all-gather(f32[20,2,2,256]{3,2,1,0:T(2,128)S(1)} %copy.58), channel_id=1, replica_groups=mesh['rec'=32,'src'=8] {'src'}, dimensions={0}, use_global_device_ids=true | all-gather | bytes 737280 | tf_op jit(solution)/shard_map/all_gather | solution.py:69
  194.7 1.4 fusion.38
  196.2 1.4 fusion.40
  197.6 1.5 fusion.4
  199.1 1.5 fusion.5
  200.6 1.7 pad_maximum_fusion
  202.3 5.1 copy.61
  208.2 146.3 %all-reduce.12.cloned.1.call-done = f32[640,2,2,256]{3,2,1,0:T(2,128)} async-done(((f32[640,2,2,256]{3,2,1,0:T(2,128)}), f32[640,2,2,256]{3,2,1,0:T(2,128)}) %all-reduce.12.cloned.1.call-update) | async-done | bytes 2621456
  354.5 1.1 multiply_reduce_fusion.4
  355.6 78.9 %psum.36 = f32[2]{0:T(128)S(1)} all-reduce(f32[2]{0:T(128)S(1)} %get-tuple-element.19), channel_id=1, replica_groups=mesh['rec'=32,'src'=8] {'rec','src'}, use_global_device_ids=true, to_apply=%region_5.6 | all-reduce | flops 2 | bytes 16 | tf_op jit(solution)/shard_map/psum | solution.py:40
  434.6 1.2 tile.8
  435.8 66.6 %all_to_all.10 = f32[640,2,2,256]{3,2,1,0:T(2,128)S(1)} all-to-all(f32[640,2,2,256]{3,2,1,0:T(2,128)S(1)} %bitcast.141), channel_id=1, replica_groups=mesh['rec'=32,'src'=8] {'rec'}, dimensions={0} | all-to-all | bytes 5242880 | tf_op jit(solution)/shard_map/all_to_all | solution.py:87
  502.4 0.9 fusion.73
  503.3 1.1 fusion.6
  504.4 1.1 fusion.7
  505.6 1.1 fusion.21
  506.7 1.1 fusion.19
  508.0 1.4 copy.66
  510.7 59.1 %all-reduce.14.cloned.1.call-done = f32[160,2,2,256]{3,2,1,0:T(2,128)} async-done(((f32[160,2,2,256]{3,2,1,0:T(2,128)}), f32[160,2,2,256]{3,2,1,0:T(2,128)}) %all-reduce.14.cloned.1.call-update) | async-done | bytes 655376
  569.8 0.9 constant_dynamic-slice_fusion.2
  570.9 78.5 %psum.37 = f32[2]{0:T(128)S(1)} all-reduce(f32[2]{0:T(128)S(1)} %multiply_reduce_fusion.2), channel_id=1, replica_groups=mesh['rec'=32,'src'=8] {'rec','src'}, use_global_device_ids=true, to_apply=%region_8.9 | all-reduce | flops 2 | bytes 16 | tf_op jit(solution)/shard_map/psum | solution.py:40
  649.5 14.2 %all_gather.19 = f32[160,2,2,256]{3,2,1,0:T(2,128)S(1)} all-gather(f32[20,2,2,256]{3,2,1,0:T(2,128)S(1)} %copy.68), channel_id=1, replica_groups=mesh['rec'=32,'src'=8] {'src'}, dimensions={0}, use_global_device_ids=true | all-gather | bytes 737280 | tf_op jit(solution)/shard_map/all_gather | solution.py:69
  663.9 1.4 fusion.32
  665.4 1.4 fusion.34
  666.8 1.5 fusion.2
  668.3 1.5 fusion.3
  669.8 1.7 pad_maximum_fusion.1
  671.5 5.1 copy.71
  676.7 147.8 %all-reduce.16.cloned.1.call-done = f32[640,2,2,256]{3,2,1,0:T(2,128)} async-done(((f32[640,2,2,256]{3,2,1,0:T(2,128)}), f32[640,2,2,256]{3,2,1,0:T(2,128)}) %all-reduce.16.cloned.1.call-update) | async-done | bytes 2621456
  824.5 0.9 constant_dynamic-slice_fusion.1
  825.6 78.4 %psum.38 = f32[2]{0:T(128)S(1)} all-reduce(f32[2]{0:T(128)S(1)} %multiply_reduce_fusion.1), channel_id=1, replica_groups=mesh['rec'=32,'src'=8] {'rec','src'}, use_global_device_ids=true, to_apply=%region_11.12 | all-reduce | flops 2 | bytes 16 | tf_op jit(solution)/shard_map/psum | solution.py:40
  904.1 1.2 tile.20
  905.3 66.8 %all_to_all.11 = f32[640,2,2,256]{3,2,1,0:T(2,128)S(1)} all-to-all(f32[640,2,2,256]{3,2,1,0:T(2,128)S(1)} %bitcast.142), channel_id=1, replica_groups=mesh['rec'=32,'src'=8] {'rec'}, dimensions={0} | all-to-all | bytes 5242880 | tf_op jit(solution)/shard_map/all_to_all | solution.py:87
  972.1 0.9 fusion.72
  973.0 1.1 fusion.10
  974.1 1.1 fusion.11
  975.3 1.1 fusion.17
  976.4 1.1 fusion.15
  977.7 1.4 copy.76
  979.0 60.4 %all-reduce.18.cloned.1.call-done = f32[160,2,2,256]{3,2,1,0:T(2,128)} async-done(((f32[160,2,2,256]{3,2,1,0:T(2,128)}), f32[160,2,2,256]{3,2,1,0:T(2,128)}) %all-reduce.18.cloned.1.call-update) | async-done | bytes 655376
  1039.5 0.9 constant_dynamic-slice_fusion
  1040.6 78.5 %psum.39 = f32[2]{0:T(128)S(1)} all-reduce(f32[2]{0:T(128)S(1)} %get-tuple-element.17), channel_id=1, replica_groups=mesh['rec'=32,'src'=8] {'rec','src'}, use_global_device_ids=true, to_apply=%region_14.15 | all-reduce | flops 2 | bytes 16 | tf_op jit(solution)/shard_map/psum | solution.py:40
  (49 shorter events, 6.3 us)
Async XLA Ops:
  7.2 85.0 %all-gather.2.cloned.1.call-start = ((), (), s32[]{:S(2)}) async-start(), calls=%async_computation.2 | async-start | bytes 3784704 | tf_op jit(solution)/shard_map/all_gather | solution.py:51
  7.9 346.6 %all-reduce.12.cloned.1.call-start = ((), (), s32[]{:S(2)}) async-start(), calls=%async_computation.3 | async-start | bytes 5242880
  102.7 92.0 %copy-start = (f32[2,2,160,640]{3,2,1,0:T(8,128)S(1)}, f32[2,2,160,640]{3,2,1,0:T(8,128)}, u32[]{:S(2)}) copy-start(f32[2,2,160,640]{3,2,1,0:T(8,128)} %param.4) | copy-start | bytes 4915204
  207.5 362.3 %all-reduce.14.cloned.1.call-start = ((), (), s32[]{:S(2)}) async-start(), calls=%async_computation.4 | async-start | bytes 1310720
  508.0 1.5 copy-start.1
  509.4 315.1 %all-reduce.16.cloned.1.call-start = ((), (), s32[]{:S(2)}) async-start(), calls=%async_computation.5 | async-start | bytes 5242880
  676.7 362.8 %all-reduce.18.cloned.1.call-start = ((), (), s32[]{:S(2)}) async-start(), calls=%async_computation.6 | async-start | bytes 1310720
Sparse Core Ops, SparseCore 0:
  10.6 81.5 all-gather.1
  207.6 146.8 all-reduce.11
  509.5 60.2 all-reduce.13
  676.8 147.6 all-reduce.15
  979.2 60.2 all-reduce.17
